TPU v7x, 32 devices: a whole 2x2x4 slice. The times are simulated.
32 devices in a mesh: layer: 8 (over y, x, core), dp: 4 (over z).
Axes of the slice: x: 2, y: 2, z: 4, core: 2. Of those that a mesh axis runs over, the one named last changes fastest.
Arguments:
- resid_in: bfloat16 [4, 128, 3584], P(None, 'dp'), may hold values from -6 to 6
- resid_out: bfloat16 [4, 128, 3584], P(None, ('layer', 'dp')), may hold values from -4 to 4
- encoder: bfloat16 [2, 3584, 32768], P(None, None, ('layer', 'dp')), may hold values from -0.09375 to 0.09375
- enc_bias: float32 [2, 32768], P(None, ('layer', 'dp')), may hold values from -3 to 3
- decoder: bfloat16 [5, 32768, 3584], P(None, ('layer', 'dp')), may hold values from -0.046875 to 0.046875
- active: int32 [4, 4, 32], replicated, may hold values from 0 to 127, all different within a row
Outputs:
- recon: bfloat16 [4, 128, 3584], P(None, ('layer', 'dp'))
- grad_encoder: bfloat16 [2, 3584, 32768], P(None, None, ('layer', 'dp'))
- grad_bias: float32 [2, 32768], P(None, ('layer', 'dp'))
- grad_decoder: bfloat16 [5, 32768, 3584], P(None, ('layer', 'dp'))
Inputs may be any that keep to these rules, and one draw needn't show every extreme that they name: Row active[l, n] lists 32 different blocks of layer l, active for tokens n * 32 to (n + 1) * 32 - 1; every block number appears in at least one row of active, counting the rows of all layers together (not necessarily in a row of every layer).
All inputs are finite; a program needn't handle non-finite values.
Results may differ from a plain program's by a relative error of at most 0.0059.
Values may be sent and summed in bfloat16 or wider, within the bound.
A program may use at most 192 MiB of HBM per device.

v0:
```python
import jax
import jax.numpy as jnp
from jax import lax
from jax.sharding import PartitionSpec as P

FEAT = 16384
BLOCK = 128
LAYERS = 4


def per_device(resid_in, resid_out, encoder, enc_bias, decoder, active):
    tok_dev = resid_in.shape[1]
    model_width = resid_in.shape[2]
    local_width = encoder.shape[2]
    dp_count = lax.axis_size("dp")
    all_count = lax.axis_size("layer") * dp_count
    device_rank = lax.axis_index("layer") * dp_count + lax.axis_index("dp")
    first_column = device_rank * local_width
    fold_side = first_column // FEAT
    offset = first_column - fold_side * FEAT
    targets = lax.all_gather(resid_out, ("layer", "dp"), axis=1, tiled=True)
    layer_ids = [fold_side, LAYERS - 1 - fold_side]
    picked = jnp.stack(
        [lax.dynamic_index_in_dim(resid_in, layer_id, 0, keepdims=False) for layer_id in layer_ids]
    )
    inputs = lax.all_gather(picked, "dp", axis=1, tiled=True)
    tokens = inputs.shape[1]
    pre_acts = (
        jnp.einsum("krd,kdf->krf", inputs, encoder, preferred_element_type=jnp.float32)
        + enc_bias[:, None, :]
    )
    block_ids = offset // BLOCK + jnp.arange(local_width // BLOCK, dtype=jnp.int32)
    block_masks = []
    for layer_id in layer_ids:
        listed = lax.dynamic_index_in_dim(active, layer_id, 0, keepdims=False)
        listed_hit = jnp.any(listed[:, :, None] == block_ids[None, None, :], axis=1).astype(
            jnp.float32
        )
        spread = jnp.broadcast_to(
            listed_hit[:, None, :, None], (listed_hit.shape[0], tok_dev, listed_hit.shape[1], BLOCK)
        )
        block_masks.append(spread.reshape(tokens, local_width))
    block_keep = jnp.stack(block_masks)
    positive = jnp.maximum(pre_acts, 0.0)
    feature_codes = (block_keep * positive * positive).astype(jnp.bfloat16)
    pair_table = []
    for pair_slot in range(decoder.shape[0]):
        second = pair_slot >= LAYERS - fold_side
        pair_table.append(
            (second.astype(jnp.int32), jnp.where(second, pair_slot - 1, fold_side + pair_slot))
        )
    decoded = jnp.zeros((LAYERS, tokens, model_width), jnp.float32)
    for pair_slot in range(decoder.shape[0]):
        source_slot, target_layer = pair_table[pair_slot]
        source_codes = lax.dynamic_index_in_dim(feature_codes, source_slot, 0, keepdims=False)
        decoded_part = jnp.dot(source_codes, decoder[pair_slot], preferred_element_type=jnp.float32)
        current = lax.dynamic_index_in_dim(decoded, target_layer, 0, keepdims=False)
        decoded = lax.dynamic_update_index_in_dim(decoded, current + decoded_part, target_layer, 0)
    totals = lax.psum(decoded, ("layer", "dp"))
    share = tokens // all_count
    recon = lax.dynamic_slice_in_dim(totals, device_rank * share, share, 1).astype(jnp.bfloat16)
    errors_all = (totals - targets.astype(jnp.float32)).astype(jnp.bfloat16)
    grad_parts = []
    back_codes = jnp.zeros((2, tokens, local_width), jnp.float32)
    for pair_slot in range(decoder.shape[0]):
        source_slot, target_layer = pair_table[pair_slot]
        source_codes = lax.dynamic_index_in_dim(feature_codes, source_slot, 0, keepdims=False)
        target_errors = lax.dynamic_index_in_dim(errors_all, target_layer, 0, keepdims=False)
        grad_parts.append(
            lax.dot_general(
                source_codes,
                target_errors,
                (((0,), (0,)), ((), ())),
                preferred_element_type=jnp.float32,
            ).astype(jnp.bfloat16)
        )
        pulled = lax.dot_general(
            target_errors,
            decoder[pair_slot],
            (((1,), (1,)), ((), ())),
            preferred_element_type=jnp.float32,
        )
        current = lax.dynamic_index_in_dim(back_codes, source_slot, 0, keepdims=False)
        back_codes = lax.dynamic_update_index_in_dim(back_codes, current + pulled, source_slot, 0)
    grad_decoder = jnp.stack(grad_parts)
    back_pre = (back_codes * block_keep * (2.0 * positive)).astype(jnp.bfloat16)
    grad_encoder = jnp.einsum(
        "krd,krf->kdf", inputs, back_pre, preferred_element_type=jnp.float32
    ).astype(jnp.bfloat16)
    grad_bias = jnp.sum(back_pre.astype(jnp.float32), axis=1)
    return (recon, grad_encoder, grad_bias, grad_decoder)


def solution(mesh):
    in_specs = (
        P(None, "dp", None),
        P(None, ("layer", "dp"), None),
        P(None, None, ("layer", "dp")),
        P(None, ("layer", "dp")),
        P(None, ("layer", "dp"), None),
        P(),
    )
    out_specs = (
        P(None, ("layer", "dp"), None),
        P(None, None, ("layer", "dp")),
        P(None, ("layer", "dp")),
        P(None, ("layer", "dp"), None),
    )
    return jax.shard_map(
        per_device, mesh=mesh, in_specs=in_specs, out_specs=out_specs, check_vma=False
    )
```

profile of v0, /device:TPU:0, one launch (start us, length us, event | category | flops | bytes accessed | tf_op | source)
XLA Modules:
  0.0 404.9 jit_solution(1773918791542335406)
XLA Ops:
  7.2 0.0 copy-start.2
  7.2 0.0 all-gather.3.cloned.1.call-start
  7.3 1.1 constant_dynamic-slice_fusion.9
  8.3 0.8 pad_maximum_fusion
  9.1 0.0 all-gather.3.cloned.1.call-update
  9.2 0.0 all-reduce.2.cloned.1.call-start
  9.3 0.7 fusion.171
  10.0 0.3 compare_reduce_fusion
  10.3 0.1 broadcast_in_dim.53
  10.4 0.1 stack_reshape.6
  10.5 0.1 broadcast_in_dim.54
  10.6 0.1 stack_reshape.7
  10.9 43.4 %all-gather.3.cloned.1.call-done = bf16[2,128,3584]{2,1,0:T(8,128)(2,1)} async-done(((bf16[2,32,3584]{2,1,0:T(8,128)(2,1)}), bf16[2,128,3584]{2,1,0:T(8,128)(2,1)}) %all-gather.3.cloned.1.call-update) | async-done | bytes 1835024 | tf_op jit(solution)/shard_map/all_gather | solution.py:26
  54.2 0.0 copy-done.2
  54.2 8.0 %fusion.115 = (bf16[2,128,1024]{2,1,0:T(8,128)(2,1)S(1)}, f32[2,128,1024]{2,1,0:T(8,128)S(1)}) fusion(f32[2,128,1024]{2,1,0:T(8,128)S(1)} %constant_dynamic-update-slice_fusion, f32[2,1024]{1,0:T(2,128)S(1)} %copy-done.2, bf16[2,128,3584]{2,1,0:T(8,128)(2,1)} %all-gather.3.cloned.1.call-done, bf16[2,3584,1024]{2,1,0:T(8,128)(2,1)} %param.8), kind=kOutput, calls=%fused_computation.73 | convolution fusion | flops 1880358912 | bytes 19144704 | tf_op jit(solution)/shard_map/krd,kdf->krf/dot_general | solution.py:29
  62.2 3.9 broadcast_in_dim.52
  66.1 5.4 %fusion.33 = f32[4,128,3584]{2,1,0:T(8,128)} fusion(f32[4,128,3584]{2,1,0:T(8,128)} %broadcast_in_dim.52, s32[]{:T(128)S(6)} %select_n.104, bf16[5,1024,3584]{2,1,0:T(8,128)(2,1)} %param.10, bf16[2,128,1024]{2,1,0:T(8,128)(2,1)S(1)} %get-tuple-element.16, s32[]{:T(128)S(6)} %select_n.102), kind=kOutput, calls=%fused_computation.43 | convolution fusion | flops 939524096 | bytes 9437192 | tf_op jit(solution)/shard_map/dot_general | solution.py:56
  71.6 1.6 constant_dynamic-slice_fusion.7
  73.2 5.5 %fusion.42 = f32[4,128,3584]{2,1,0:T(8,128)} fusion(f32[4,128,3584]{2,1,0:T(8,128)} %fusion.33, s32[]{:T(128)S(6)} %select_n.106, bf16[5,1024,3584]{2,1,0:T(8,128)(2,1)} %param.10, f32[1,128,3584]{2,1,0:T(8,128)S(1)} %constant_dynamic-slice_fusion.7, bf16[2,128,1024]{2,1,0:T(8,128)(2,1)S(1)} %get-tuple-element.16, s32[]{:T(128)S(6)} %select_n.107), kind=kOutput, calls=%fused_computation.46 | convolution fusion | flops 939982848 | bytes 11272200 | tf_op jit(solution)/shard_map/dot_general | solution.py:56
  78.7 1.6 constant_dynamic-slice_fusion.6
  80.3 5.5 %fusion.51 = f32[4,128,3584]{2,1,0:T(8,128)} fusion(f32[4,128,3584]{2,1,0:T(8,128)} %fusion.42, s32[]{:T(128)S(6)} %select_n.109, bf16[5,1024,3584]{2,1,0:T(8,128)(2,1)} %param.10, f32[1,128,3584]{2,1,0:T(8,128)S(1)} %constant_dynamic-slice_fusion.6, bf16[2,128,1024]{2,1,0:T(8,128)(2,1)S(1)} %get-tuple-element.16, s32[]{:T(128)S(6)} %select_n.110), kind=kOutput, calls=%fused_computation.49 | convolution fusion | flops 939982848 | bytes 11272200 | tf_op jit(solution)/shard_map/dot_general | solution.py:56
  85.8 1.6 constant_dynamic-slice_fusion.4
  87.4 5.5 %fusion.60 = f32[4,128,3584]{2,1,0:T(8,128)} fusion(f32[4,128,3584]{2,1,0:T(8,128)} %fusion.51, s32[]{:T(128)S(6)} %select_n.112, bf16[5,1024,3584]{2,1,0:T(8,128)(2,1)} %param.10, f32[1,128,3584]{2,1,0:T(8,128)S(1)} %constant_dynamic-slice_fusion.4, bf16[2,128,1024]{2,1,0:T(8,128)(2,1)S(1)} %get-tuple-element.16, s32[]{:T(128)S(6)} %select_n.113), kind=kOutput, calls=%fused_computation.52 | convolution fusion | flops 939982848 | bytes 11272200 | tf_op jit(solution)/shard_map/dot_general | solution.py:56
  92.9 1.6 constant_dynamic-slice_fusion.3
  94.5 0.0 copy-start.1
  94.5 5.5 %fusion.69 = f32[4,128,3584]{2,1,0:T(8,128)} fusion(f32[4,128,3584]{2,1,0:T(8,128)} %fusion.60, s32[]{:T(128)S(6)} %select_n.115, bf16[5,1024,3584]{2,1,0:T(8,128)(2,1)} %param.10, f32[1,128,3584]{2,1,0:T(8,128)S(1)} %constant_dynamic-slice_fusion.3, bf16[2,128,1024]{2,1,0:T(8,128)(2,1)S(1)} %get-tuple-element.16, s32[]{:T(128)S(6)} %select_n.116), kind=kOutput, calls=%fused_computation.55 | convolution fusion | flops 939982848 | bytes 11272200 | tf_op jit(solution)/shard_map/dot_general | solution.py:56
  100.0 0.0 all-reduce.2.cloned.1.call-update
  100.0 0.2 all-gather.5.cloned.1.call-start
  100.3 0.0 copy-done.1
  100.3 0.7 copy.19
  101.0 0.0 all-gather.5.cloned.1.call-update
  101.0 165.3 %all-reduce.2.cloned.1.call-done = f32[4,128,3584]{2,1,0:T(8,128)} async-done(((f32[4,128,3584]{2,1,0:T(8,128)}), f32[4,128,3584]{2,1,0:T(8,128)}) %all-reduce.2.cloned.1.call-update) | async-done | bytes 7340048 | tf_op jit(solution)/shard_map/psum | solution.py:59
  266.3 1.7 dynamic-slice_convert_fusion
  268.0 62.2 %all-gather.5.cloned.1.call-done = bf16[4,128,3584]{2,0,1:T(4,128)(2,1)} async-done(((bf16[4,4,3584]{2,0,1:T(4,128)(2,1)}), bf16[4,128,3584]{2,0,1:T(4,128)(2,1)}) %all-gather.5.cloned.1.call-update) | async-done | bytes 3670032 | tf_op jit(solution)/shard_map/all_gather | solution.py:21
  330.3 5.5 %subtract_convert_fusion = bf16[4,128,3584]{2,1,0:T(8,128)(2,1)S(1)} fusion(f32[4,128,3584]{2,1,0:T(8,128)} %all-reduce.2.cloned.1.call-done, bf16[4,128,3584]{2,0,1:T(4,128)(2,1)} %all-gather.5.cloned.1.call-done), kind=kLoop, calls=%fused_computation.31 | loop fusion | flops 5505024 | bytes 14680064 | tf_op jit(solution)/shard_map/convert_element_type | solution.py:62
  335.7 5.2 %bitcast_dynamic-update-slice_fusion.4 = bf16[5,1024,3584]{2,1,0:T(8,128)(2,1)} fusion(bf16[4,128,3584]{2,1,0:T(8,128)(2,1)S(1)} %subtract_convert_fusion, s32[]{:T(128)S(6)} %select_n.104, bf16[2,128,1024]{2,1,0:T(8,128)(2,1)S(1)} %get-tuple-element.16, s32[]{:T(128)S(6)} %select_n.102), kind=kOutput, calls=%fused_computation.10 | convolution fusion | flops 943194112 | bytes 8519688 | tf_op jit(solution)/shard_map/dot_general | solution.py:70
  340.9 5.1 %bitcast_dynamic-update-slice_fusion.3 = bf16[5,1024,3584]{2,1,0:T(8,128)(2,1)} fusion(bf16[5,1024,3584]{2,1,0:T(8,128)(2,1)} %bitcast_dynamic-update-slice_fusion.4, bf16[4,128,3584]{2,1,0:T(8,128)(2,1)S(1)} %subtract_convert_fusion, s32[]{:T(128)S(6)} %select_n.106, bf16[2,128,1024]{2,1,0:T(8,128)(2,1)S(1)} %get-tuple-element.16, s32[]{:T(128)S(6)} %select_n.107), kind=kOutput, calls=%fused_computation.9 | convolution fusion | flops 943194112 | bytes 8519688 | tf_op jit(solution)/shard_map/dot_general | solution.py:70
  346.0 5.1 %bitcast_dynamic-update-slice_fusion.2 = bf16[5,1024,3584]{2,1,0:T(8,128)(2,1)} fusion(bf16[5,1024,3584]{2,1,0:T(8,128)(2,1)} %bitcast_dynamic-update-slice_fusion.3, bf16[4,128,3584]{2,1,0:T(8,128)(2,1)S(1)} %subtract_convert_fusion, s32[]{:T(128)S(6)} %select_n.109, bf16[2,128,1024]{2,1,0:T(8,128)(2,1)S(1)} %get-tuple-element.16, s32[]{:T(128)S(6)} %select_n.110), kind=kOutput, calls=%fused_computation.8 | convolution fusion | flops 943194112 | bytes 8519688 | tf_op jit(solution)/shard_map/dot_general | solution.py:70
  351.2 5.1 %bitcast_dynamic-update-slice_fusion.1 = bf16[5,1024,3584]{2,1,0:T(8,128)(2,1)} fusion(bf16[5,1024,3584]{2,1,0:T(8,128)(2,1)} %bitcast_dynamic-update-slice_fusion.2, bf16[4,128,3584]{2,1,0:T(8,128)(2,1)S(1)} %subtract_convert_fusion, s32[]{:T(128)S(6)} %select_n.112, bf16[2,128,1024]{2,1,0:T(8,128)(2,1)S(1)} %get-tuple-element.16, s32[]{:T(128)S(6)} %select_n.113), kind=kOutput, calls=%fused_computation.7 | convolution fusion | flops 943194112 | bytes 8519688 | tf_op jit(solution)/shard_map/dot_general | solution.py:70
  356.3 5.1 %bitcast_dynamic-update-slice_fusion = bf16[5,1024,3584]{2,1,0:T(8,128)(2,1)} fusion(bf16[5,1024,3584]{2,1,0:T(8,128)(2,1)} %bitcast_dynamic-update-slice_fusion.1, bf16[4,128,3584]{2,1,0:T(8,128)(2,1)S(1)} %subtract_convert_fusion, s32[]{:T(128)S(6)} %select_n.115, bf16[2,128,1024]{2,1,0:T(8,128)(2,1)S(1)} %get-tuple-element.16, s32[]{:T(128)S(6)} %select_n.116), kind=kOutput, calls=%fused_computation.6 | convolution fusion | flops 943194112 | bytes 8519688 | tf_op jit(solution)/shard_map/dot_general | solution.py:70
  361.5 0.1 broadcast.16
  361.6 5.7 %fusion.76 = f32[2,128,1024]{2,1,0:T(8,128)S(1)} fusion(f32[2,128,1024]{2,1,0:T(8,128)S(1)} %broadcast.16, s32[]{:T(128)S(6)} %select_n.102, bf16[5,1024,3584]{2,1,0:T(8,128)(2,1)} %param.10, bf16[4,128,3584]{2,1,0:T(8,128)(2,1)S(1)} %subtract_convert_fusion, s32[]{:T(128)S(6)} %select_n.104), kind=kOutput, calls=%fused_computation.60 | convolution fusion | flops 939524096 | bytes 8781832 | tf_op jit(solution)/shard_map/dot_general | solution.py:77
  367.4 5.5 %fusion.85 = f32[2,128,1024]{2,1,0:T(8,128)S(1)} fusion(f32[2,128,1024]{2,1,0:T(8,128)S(1)} %fusion.76, s32[]{:T(128)S(6)} %select_n.107, bf16[5,1024,3584]{2,1,0:T(8,128)(2,1)} %param.10, bf16[4,128,3584]{2,1,0:T(8,128)(2,1)S(1)} %subtract_convert_fusion, s32[]{:T(128)S(6)} %select_n.106, f32[1,128,1024]{2,1,0:T(8,128)S(1)} %constant_dynamic-slice_fusion.2), kind=kOutput, calls=%fused_computation.63 | convolution fusion | flops 939655168 | bytes 9306120 | tf_op jit(solution)/shard_map/dot_general | solution.py:77
  373.0 5.5 %fusion.94 = f32[2,128,1024]{2,1,0:T(8,128)S(1)} fusion(f32[2,128,1024]{2,1,0:T(8,128)S(1)} %fusion.85, s32[]{:T(128)S(6)} %select_n.110, bf16[5,1024,3584]{2,1,0:T(8,128)(2,1)} %param.10, bf16[4,128,3584]{2,1,0:T(8,128)(2,1)S(1)} %subtract_convert_fusion, s32[]{:T(128)S(6)} %select_n.109, f32[1,128,1024]{2,1,0:T(8,128)S(1)} %constant_dynamic-slice_fusion.1), kind=kOutput, calls=%fused_computation.66 | convolution fusion | flops 939655168 | bytes 9306120 | tf_op jit(solution)/shard_map/dot_general | solution.py:77
  378.6 5.5 %fusion.103 = f32[2,128,1024]{2,1,0:T(8,128)S(1)} fusion(f32[2,128,1024]{2,1,0:T(8,128)S(1)} %fusion.94, s32[]{:T(128)S(6)} %select_n.113, bf16[5,1024,3584]{2,1,0:T(8,128)(2,1)} %param.10, bf16[4,128,3584]{2,1,0:T(8,128)(2,1)S(1)} %subtract_convert_fusion, s32[]{:T(128)S(6)} %select_n.112, f32[1,128,1024]{2,1,0:T(8,128)S(1)} %constant_dynamic-slice_fusion), kind=kOutput, calls=%fused_computation.69 | convolution fusion | flops 939655168 | bytes 9306120 | tf_op jit(solution)/shard_map/dot_general | solution.py:77
  384.2 0.0 copy-start
  384.2 5.7 %fusion.112 = f32[2,128,1024]{2,1,0:T(8,128)S(1)} fusion(f32[2,128,1024]{2,1,0:T(8,128)S(1)} %fusion.103, s32[]{:T(128)S(6)} %select_n.116, bf16[5,1024,3584]{2,1,0:T(8,128)(2,1)} %param.10, bf16[4,128,3584]{2,1,0:T(8,128)(2,1)S(1)} %subtract_convert_fusion, s32[]{:T(128)S(6)} %select_n.115, f32[1,128,1024]{2,1,0:T(8,128)S(1)} %constant_dynamic-slice_fusion.5), kind=kOutput, calls=%fused_computation.72 | convolution fusion | flops 939655168 | bytes 9306120 | tf_op jit(solution)/shard_map/dot_general | solution.py:77
  389.9 1.0 convert_reduce_fusion
  390.8 0.0 copy-done
  390.8 7.6 %convolution_convert_fusion = bf16[2,3584,1024]{2,1,0:T(8,128)(2,1)} fusion(bf16[2,128,3584]{2,1,0:T(8,128)(2,1)S(1)} %copy-done, bf16[2,128,1024]{2,1,0:T(8,128)(2,1)S(1)} %get-tuple-element.11), kind=kOutput, calls=%fused_computation | convolution fusion | flops 1886388224 | bytes 17039360 | tf_op jit(solution)/shard_map/krd,krf->kdf/dot_general | solution.py:87
  (9 shorter events, 0.3 us)
Async XLA Ops:
  7.2 47.1 %copy-start.2 = (f32[2,1024]{1,0:T(2,128)S(1)}, f32[2,1024]{1,0:T(2,128)}, u32[]{:S(2)}) copy-start(f32[2,1024]{1,0:T(2,128)} %param.9) | copy-start | bytes 24580
  7.2 47.0 %all-gather.3.cloned.1.call-start = ((), (), s32[]{:S(2)}) async-start(), calls=%async_computation | async-start | bytes 2293760 | tf_op jit(solution)/shard_map/all_gather | solution.py:26
  9.2 257.1 %all-reduce.2.cloned.1.call-start = ((), (), s32[]{:S(2)}) async-start(), calls=%async_computation.1 | async-start | bytes 14680064 | tf_op jit(solution)/shard_map/psum | solution.py:59
  94.5 5.8 %copy-start.1 = (bf16[4,4,3584]{2,1,0:T(4,128)(2,1)S(1)}, bf16[4,4,3584]{2,1,0:T(4,128)(2,1)}, u32[]{:S(2)}) copy-start(bf16[4,4,3584]{2,1,0:T(4,128)(2,1)} %param.7) | copy-start | bytes 344068
  100.0 230.2 %all-gather.5.cloned.1.call-start = ((), (), s32[]{:S(2)}) async-start(), calls=%async_computation.2 | async-start | bytes 3784704 | tf_op jit(solution)/shard_map/all_gather | solution.py:21
  384.2 6.6 %copy-start = (bf16[2,128,3584]{2,1,0:T(8,128)(2,1)S(1)}, bf16[2,128,3584]{2,1,0:T(8,128)(2,1)}, u32[]{:S(2)}) copy-start(bf16[2,128,3584]{2,1,0:T(8,128)(2,1)} %all-gather.3.cloned.1.call-done) | copy-start | bytes 5505028
Sparse Core Ops, SparseCore 0:
  10.1 44.0 all-gather.2
  100.2 166.0 all-reduce.1
  269.7 60.4 all-gather.4
where the time goes:
time: 406 us; the launch traced here: 405 us
  waiting for transfers between devices  271 us (67%)
  matrix products  96.6 us (24%)
  local copies, waits for them, and re-layouts  15.4 us (4%)
  between operations  14.1 us (3%)
  other arithmetic  7.55 us (2%)
    psum x1, waiting for transfers between devices, per_device(): totals = lax.psum(decoded, ('layer', 'dp'))  165 us
    all_gather x1, waiting for transfers between devices, per_device(): targets = lax.all_gather(resid_out, ('layer', 'dp'), axis=1, tiled=True)  62.2 us
    all_gather x1, waiting for transfers between devices, per_device(): inputs = lax.all_gather(picked, 'dp', axis=1, tiled=True)  43.4 us
    dot_general x5, matrix products, per_device(): lax.dot_general(target_errors, decoder[pair_slot], (((1,), (1,)), ((), ()...  28 us
    dot_general x5, matrix products, per_device(): jnp.dot(source_codes, decoder[pair_slot], preferred_element_type=jnp.floa...  27.3 us
    dot_general x5, matrix products, per_device(): lax.dot_general(source_codes, target_errors, (((0,), (0,)), ((), ())), pr...  25.7 us
  transfers between devices with their start and end apart: 3, of which 3 were waited for; matrix products, arithmetic and copies ran while one was open for 1% of the time, Pallas kernels for 0%

commit v1 on v0

--- a/solution.py
+++ b/solution.py
@@ -23,7 +23,12 @@
     picked = jnp.stack(
         [lax.dynamic_index_in_dim(resid_in, layer_id, 0, keepdims=False) for layer_id in layer_ids]
     )
-    inputs = lax.all_gather(picked, "dp", axis=1, tiled=True)
+    ring = [picked]
+    for hop in range(3):
+        ring.append(lax.ppermute(ring[-1], "dp", [(dev, (dev + 1) % 4) for dev in range(4)]))
+    inputs = jnp.roll(
+        jnp.concatenate(ring[::-1], axis=1), (lax.axis_index("dp") + 1) * ring[0].shape[1], axis=1
+    )
     tokens = inputs.shape[1]
     pre_acts = (
         jnp.einsum("krd,kdf->krf", inputs, encoder, preferred_element_type=jnp.float32)

time: 406 us -> 413 us (1.017)
  local copies, waits for them, and re-layouts: 15.4 us -> 26.6 us
  waiting for transfers between devices: 271 us -> 264 us
    all_gather x1 -> x0, waiting for transfers between devices: 43.4 us -> none  [per_device(): inputs = lax.all_gather(picked, 'dp', axis=1, tiled=True)]
    ppermute x0 -> x3, waiting for transfers between devices: none -> 37.5 us  [per_device(): lax.ppermute(ring[-1], 'dp', [(dev, (dev + 1) % 4) for dev in range(4)])]
    unnamed x8 -> x40, local copies, waits for them, and re-layouts: 0.75 us -> 6.23 us
    dynamic_slice x4, local copies, waits for them, and re-layouts: 6.5 us -> 11.6 us  [per_device(): current = lax.dynamic_index_in_dim(decoded, target_layer, 0, keepdims=False)]
  transfers between devices with their start and end apart: 3 -> 5, of which waited for: 3 -> 5; matrix products, arithmetic and copies ran while one was open for 1% -> 1% of each run, Pallas kernels for 0% -> 0%
where the time goes in v1:
time: 413 us; the launch traced here: 412 us
  waiting for transfers between devices  264 us (64%)
  matrix products  95.7 us (23%)
  local copies, waits for them, and re-layouts  26.6 us (6%)
  between operations  14.5 us (4%)
  other arithmetic  7.65 us (2%)
    psum x1, waiting for transfers between devices, per_device(): totals = lax.psum(decoded, ('layer', 'dp'))  164 us
    all_gather x1, waiting for transfers between devices, per_device(): targets = lax.all_gather(resid_out, ('layer', 'dp'), axis=1, tiled=True)  62.2 us
    ppermute x3, waiting for transfers between devices, per_device(): lax.ppermute(ring[-1], 'dp', [(dev, (dev + 1) % 4) for dev in range(4)])  37.5 us
    dot_general x5, matrix products, per_device(): lax.dot_general(target_errors, decoder[pair_slot], (((1,), (1,)), ((), ()...  28 us
    dot_general x5, matrix products, per_device(): lax.dot_general(source_codes, target_errors, (((0,), (0,)), ((), ())), pr...  25.7 us
    dot_general x5, matrix products, per_device(): jnp.dot(source_codes, decoder[pair_slot], preferred_element_type=jnp.floa...  23.3 us
    dynamic_slice x4, local copies, waits for them, and re-layouts, per_device(): current = lax.dynamic_index_in_dim(decoded, target_layer, 0, keepdims=False)  11.6 us
    dot_general x1, matrix products, per_device(): jnp.einsum('krd,kdf->krf', inputs, encoder, preferred_element_type=jnp.fl...  9.98 us
  transfers between devices with their start and end apart: 5, of which 5 were waited for; matrix products, arithmetic and copies ran while one was open for 1% of the time, Pallas kernels for 0%

profile of v1, /device:TPU:0, one launch (start us, length us, event | category | flops | bytes accessed | tf_op | source)
XLA Modules:
  0.0 411.8 jit_solution(9315381056684367082)
XLA Ops:
  7.2 0.0 copy-start.6
  7.2 0.0 all-reduce.2.cloned.1.call-start
  7.3 1.1 constant_dynamic-slice_fusion.9
  8.4 3.1 collective-permute-start
  11.5 12.5 %collective-permute-done = bf16[2,32,3584]{2,1,0:T(8,128)(2,1)S(1)} collective-permute-done((bf16[2,32,3584]{2,1,0:T(8,128)(2,1)S(1)}, bf16[2,32,3584]{2,1,0:T(8,128)(2,1)S(1)}, u32[]{:S(2)}, u32[]{:S(2)}) %collective-permute-start) | collective-permute-done | bytes 458784 | tf_op jit(solution)/shard_map/ppermute | solution.py:28
  24.0 0.0 collective-permute-start.1
  24.0 0.7 fusion.181
  24.8 12.8 %collective-permute-done.1 = bf16[2,32,3584]{2,1,0:T(8,128)(2,1)} collective-permute-done((bf16[2,32,3584]{2,1,0:T(8,128)(2,1)S(1)}, bf16[2,32,3584]{2,1,0:T(8,128)(2,1)}, u32[]{:S(2)}, u32[]{:S(2)}) %collective-permute-start.1) | collective-permute-done | bytes 458784 | tf_op jit(solution)/shard_map/ppermute | solution.py:28
  37.6 0.0 collective-permute-start.2
  37.6 0.3 compare_reduce_fusion
  37.9 0.0 copy-done.3
  37.9 0.1 broadcast_in_dim.53
  38.1 0.1 stack_reshape.6
  38.2 0.1 broadcast_in_dim.54
  38.3 0.1 stack_reshape.7
  38.4 0.0 copy-start.4
  38.5 12.1 %collective-permute-done.2 = bf16[2,32,3584]{2,1,0:T(8,128)(2,1)} collective-permute-done((bf16[2,32,3584]{2,1,0:T(8,128)(2,1)}, bf16[2,32,3584]{2,1,0:T(8,128)(2,1)}, u32[]{:S(2)}, u32[]{:S(2)}) %collective-permute-start.2) | collective-permute-done | bytes 458784 | tf_op jit(solution)/shard_map/ppermute | solution.py:28
  50.6 1.0 constant_dynamic-update-slice_fusion.9
  51.6 1.1 constant_dynamic-update-slice_fusion.8
  52.7 1.1 constant_dynamic-update-slice_fusion.7
  53.8 0.0 slice-start
  53.8 1.2 constant_dynamic-update-slice_fusion.5
  55.0 1.1 constant_dynamic-update-slice_fusion.4
  56.0 0.0 copy-done.4
  56.1 0.0 copy-done.6
  56.1 0.0 copy-start.1
  56.2 0.0 slice-start.1
  56.2 0.0 slice-start.2
  56.2 0.0 slice-start.3
  56.2 0.0 slice-start.4
  56.2 10.0 %fusion.123 = (bf16[2,128,1024]{2,1,0:T(8,128)(2,1)S(1)}, f32[2,128,1024]{2,1,0:T(8,128)}) fusion(f32[2,128,1024]{2,1,0:T(8,128)S(1)} %constant_dynamic-update-slice_fusion, f32[2,1024]{1,0:T(2,128)S(1)} %copy-done.6, bf16[2,3584,1024]{2,1,0:T(8,128)(2,1)} %param.8, bf16[2,256,3584]{2,1,0:T(8,128)(2,1)S(1)} %constant_dynamic-update-slice_fusion.2, ...), kind=kOutput, calls=%fused_computation.76 | convolution fusion | flops 1880358912 | bytes 19144708 | tf_op jit(solution)/shard_map/krd,kdf->krf/dot_general | solution.py:34
  66.2 0.0 copy-done.1
  66.2 4.5 %broadcast_in_dim.52 = f32[4,128,3584]{2,1,0:T(8,128)} broadcast(f32[]{:T(128)} %constant.152.clone.1), dimensions={} | broadcast | bytes 7340036 | tf_op jit(solution)/shard_map/broadcast_in_dim | solution.py:57
  70.7 5.6 %fusion.33 = f32[4,128,3584]{2,1,0:T(8,128)} fusion(f32[4,128,3584]{2,1,0:T(8,128)} %broadcast_in_dim.52, s32[]{:T(128)S(6)} %select_n.118, bf16[5,1024,3584]{2,1,0:T(8,128)(2,1)} %param.10, bf16[2,128,1024]{2,1,0:T(8,128)(2,1)S(1)} %get-tuple-element.16, s32[]{:T(128)S(6)} %select_n.116), kind=kOutput, calls=%fused_computation.43 | convolution fusion | flops 939524096 | bytes 9437192 | tf_op jit(solution)/shard_map/dot_general | solution.py:61
  76.3 3.0 constant_dynamic-slice_fusion.7
  79.3 6.1 %fusion.42 = f32[4,128,3584]{2,1,0:T(8,128)} fusion(f32[4,128,3584]{2,1,0:T(8,128)} %fusion.33, s32[]{:T(128)S(6)} %select_n.120, bf16[5,1024,3584]{2,1,0:T(8,128)(2,1)} %param.10, f32[1,128,3584]{2,1,0:T(8,128)} %constant_dynamic-slice_fusion.7, bf16[2,128,1024]{2,1,0:T(8,128)(2,1)S(1)} %get-tuple-element.16, s32[]{:T(128)S(6)} %select_n.121), kind=kOutput, calls=%fused_computation.46 | convolution fusion | flops 939982848 | bytes 11272200 | tf_op jit(solution)/shard_map/dot_general | solution.py:61
  85.4 2.9 constant_dynamic-slice_fusion.5
  88.3 0.0 slice-done
  88.4 3.9 fusion.51
  92.2 2.9 constant_dynamic-slice_fusion.4
  95.1 3.9 fusion.60
  99.0 2.9 constant_dynamic-slice_fusion.3
  101.8 3.9 fusion.69
  105.7 0.0 all-reduce.2.cloned.1.call-update
  105.8 0.2 all-gather.2.cloned.1.call-start
  106.0 0.7 copy.22
  106.7 0.0 all-gather.2.cloned.1.call-update
  106.7 164.3 %all-reduce.2.cloned.1.call-done = f32[4,128,3584]{2,1,0:T(8,128)} async-done(((f32[4,128,3584]{2,1,0:T(8,128)}), f32[4,128,3584]{2,1,0:T(8,128)}) %all-reduce.2.cloned.1.call-update) | async-done | bytes 7340048 | tf_op jit(solution)/shard_map/psum | solution.py:64
  271.0 1.7 dynamic-slice_convert_fusion
  272.7 62.2 %all-gather.2.cloned.1.call-done = bf16[4,128,3584]{2,0,1:T(4,128)(2,1)} async-done(((bf16[4,4,3584]{2,0,1:T(4,128)(2,1)}), bf16[4,128,3584]{2,0,1:T(4,128)(2,1)}) %all-gather.2.cloned.1.call-update) | async-done | bytes 3670032 | tf_op jit(solution)/shard_map/all_gather | solution.py:21
  334.9 5.5 %subtract_convert_fusion = bf16[4,128,3584]{2,1,0:T(8,128)(2,1)S(1)} fusion(f32[4,128,3584]{2,1,0:T(8,128)} %all-reduce.2.cloned.1.call-done, bf16[4,128,3584]{2,0,1:T(4,128)(2,1)} %all-gather.2.cloned.1.call-done), kind=kLoop, calls=%fused_computation.31 | loop fusion | flops 5505024 | bytes 14680064 | tf_op jit(solution)/shard_map/convert_element_type | solution.py:67
  340.4 5.2 %bitcast_dynamic-update-slice_fusion.4 = bf16[5,1024,3584]{2,1,0:T(8,128)(2,1)} fusion(bf16[4,128,3584]{2,1,0:T(8,128)(2,1)S(1)} %subtract_convert_fusion, s32[]{:T(128)S(6)} %select_n.118, bf16[2,128,1024]{2,1,0:T(8,128)(2,1)S(1)} %get-tuple-element.16, s32[]{:T(128)S(6)} %select_n.116), kind=kOutput, calls=%fused_computation.10 | convolution fusion | flops 943194112 | bytes 8519688 | tf_op jit(solution)/shard_map/dot_general | solution.py:75
  345.6 5.1 %bitcast_dynamic-update-slice_fusion.3 = bf16[5,1024,3584]{2,1,0:T(8,128)(2,1)} fusion(bf16[5,1024,3584]{2,1,0:T(8,128)(2,1)} %bitcast_dynamic-update-slice_fusion.4, bf16[4,128,3584]{2,1,0:T(8,128)(2,1)S(1)} %subtract_convert_fusion, s32[]{:T(128)S(6)} %select_n.120, bf16[2,128,1024]{2,1,0:T(8,128)(2,1)S(1)} %get-tuple-element.16, s32[]{:T(128)S(6)} %select_n.121), kind=kOutput, calls=%fused_computation.9 | convolution fusion | flops 943194112 | bytes 8519688 | tf_op jit(solution)/shard_map/dot_general | solution.py:75
  350.7 5.1 %bitcast_dynamic-update-slice_fusion.2 = bf16[5,1024,3584]{2,1,0:T(8,128)(2,1)} fusion(bf16[5,1024,3584]{2,1,0:T(8,128)(2,1)} %bitcast_dynamic-update-slice_fusion.3, bf16[4,128,3584]{2,1,0:T(8,128)(2,1)S(1)} %subtract_convert_fusion, s32[]{:T(128)S(6)} %select_n.123, bf16[2,128,1024]{2,1,0:T(8,128)(2,1)S(1)} %get-tuple-element.16, s32[]{:T(128)S(6)} %select_n.124), kind=kOutput, calls=%fused_computation.8 | convolution fusion | flops 943194112 | bytes 8519688 | tf_op jit(solution)/shard_map/dot_general | solution.py:75
  355.9 5.1 %bitcast_dynamic-update-slice_fusion.1 = bf16[5,1024,3584]{2,1,0:T(8,128)(2,1)} fusion(bf16[5,1024,3584]{2,1,0:T(8,128)(2,1)} %bitcast_dynamic-update-slice_fusion.2, bf16[4,128,3584]{2,1,0:T(8,128)(2,1)S(1)} %subtract_convert_fusion, s32[]{:T(128)S(6)} %select_n.126, bf16[2,128,1024]{2,1,0:T(8,128)(2,1)S(1)} %get-tuple-element.16, s32[]{:T(128)S(6)} %select_n.127), kind=kOutput, calls=%fused_computation.7 | convolution fusion | flops 943194112 | bytes 8519688 | tf_op jit(solution)/shard_map/dot_general | solution.py:75
  361.0 5.1 %bitcast_dynamic-update-slice_fusion = bf16[5,1024,3584]{2,1,0:T(8,128)(2,1)} fusion(bf16[5,1024,3584]{2,1,0:T(8,128)(2,1)} %bitcast_dynamic-update-slice_fusion.1, bf16[4,128,3584]{2,1,0:T(8,128)(2,1)S(1)} %subtract_convert_fusion, s32[]{:T(128)S(6)} %select_n.129, bf16[2,128,1024]{2,1,0:T(8,128)(2,1)S(1)} %get-tuple-element.16, s32[]{:T(128)S(6)} %select_n.130), kind=kOutput, calls=%fused_computation.6 | convolution fusion | flops 943194112 | bytes 8519688 | tf_op jit(solution)/shard_map/dot_general | solution.py:75
  366.2 0.1 broadcast.17
  366.3 5.7 %fusion.84 = f32[2,128,1024]{2,1,0:T(8,128)S(1)} fusion(f32[2,128,1024]{2,1,0:T(8,128)S(1)} %broadcast.17, s32[]{:T(128)S(6)} %select_n.116, bf16[5,1024,3584]{2,1,0:T(8,128)(2,1)} %param.10, bf16[4,128,3584]{2,1,0:T(8,128)(2,1)S(1)} %subtract_convert_fusion, s32[]{:T(128)S(6)} %select_n.118), kind=kOutput, calls=%fused_computation.63 | convolution fusion | flops 939524096 | bytes 8781832 | tf_op jit(solution)/shard_map/dot_general | solution.py:82
  372.1 5.5 %fusion.93 = f32[2,128,1024]{2,1,0:T(8,128)S(1)} fusion(f32[2,128,1024]{2,1,0:T(8,128)S(1)} %fusion.84, s32[]{:T(128)S(6)} %select_n.121, bf16[5,1024,3584]{2,1,0:T(8,128)(2,1)} %param.10, bf16[4,128,3584]{2,1,0:T(8,128)(2,1)S(1)} %subtract_convert_fusion, s32[]{:T(128)S(6)} %select_n.120, f32[1,128,1024]{2,1,0:T(8,128)S(1)} %constant_dynamic-slice_fusion.2), kind=kOutput, calls=%fused_computation.66 | convolution fusion | flops 939655168 | bytes 9306120 | tf_op jit(solution)/shard_map/dot_general | solution.py:82
  377.7 5.5 %fusion.102 = f32[2,128,1024]{2,1,0:T(8,128)S(1)} fusion(f32[2,128,1024]{2,1,0:T(8,128)S(1)} %fusion.93, s32[]{:T(128)S(6)} %select_n.124, bf16[5,1024,3584]{2,1,0:T(8,128)(2,1)} %param.10, bf16[4,128,3584]{2,1,0:T(8,128)(2,1)S(1)} %subtract_convert_fusion, s32[]{:T(128)S(6)} %select_n.123, f32[1,128,1024]{2,1,0:T(8,128)S(1)} %constant_dynamic-slice_fusion.1), kind=kOutput, calls=%fused_computation.69 | convolution fusion | flops 939655168 | bytes 9306120 | tf_op jit(solution)/shard_map/dot_general | solution.py:82
  383.3 5.5 %fusion.111 = f32[2,128,1024]{2,1,0:T(8,128)S(1)} fusion(f32[2,128,1024]{2,1,0:T(8,128)S(1)} %fusion.102, s32[]{:T(128)S(6)} %select_n.127, bf16[5,1024,3584]{2,1,0:T(8,128)(2,1)} %param.10, bf16[4,128,3584]{2,1,0:T(8,128)(2,1)S(1)} %subtract_convert_fusion, s32[]{:T(128)S(6)} %select_n.126, f32[1,128,1024]{2,1,0:T(8,128)S(1)} %constant_dynamic-slice_fusion), kind=kOutput, calls=%fused_computation.72 | convolution fusion | flops 939655168 | bytes 9306120 | tf_op jit(solution)/shard_map/dot_general | solution.py:82
  388.9 5.7 %fusion.120 = f32[2,128,1024]{2,1,0:T(8,128)S(1)} fusion(f32[2,128,1024]{2,1,0:T(8,128)S(1)} %fusion.111, s32[]{:T(128)S(6)} %select_n.130, bf16[5,1024,3584]{2,1,0:T(8,128)(2,1)} %param.10, bf16[4,128,3584]{2,1,0:T(8,128)(2,1)S(1)} %subtract_convert_fusion, s32[]{:T(128)S(6)} %select_n.129, f32[1,128,1024]{2,1,0:T(8,128)S(1)} %constant_dynamic-slice_fusion.6), kind=kOutput, calls=%fused_computation.75 | convolution fusion | flops 939655168 | bytes 9306120 | tf_op jit(solution)/shard_map/dot_general | solution.py:82
  394.6 1.8 convert_reduce_fusion
  396.3 8.6 %convolution_convert_fusion = bf16[2,3584,1024]{2,1,0:T(8,128)(2,1)} fusion(bf16[2,128,1024]{2,1,0:T(8,128)(2,1)} %get-tuple-element.11, bf16[2,256,3584]{2,1,0:T(8,128)(2,1)S(1)} %copy-done.2, s32[]{:T(128)S(6)} %select_n.115), kind=kOutput, calls=%fused_computation | convolution fusion | flops 1886388224 | bytes 17039364 | tf_op jit(solution)/shard_map/krd,krf->kdf/dot_general | solution.py:92
  (33 shorter events, 0.5 us)
Async XLA Ops:
  7.2 49.0 %copy-start.6 = (f32[2,1024]{1,0:T(2,128)S(1)}, f32[2,1024]{1,0:T(2,128)}, u32[]{:S(2)}) copy-start(f32[2,1024]{1,0:T(2,128)} %param.9) | copy-start | bytes 24580
  7.2 263.8 %all-reduce.2.cloned.1.call-start = ((), (), s32[]{:S(2)}) async-start(), calls=%async_computation | async-start | bytes 14680064 | tf_op jit(solution)/shard_map/psum | solution.py:64
  8.4 15.6 %collective-permute-start = (bf16[2,32,3584]{2,1,0:T(8,128)(2,1)S(1)}, bf16[2,32,3584]{2,1,0:T(8,128)(2,1)S(1)}, u32[]{:S(2)}, u32[]{:S(2)}) collective-permute-start(bf16[2,32,3584]{2,1,0:T(8,128)(2,1)S(1)} %pad_maximum_fusion), channel_id=1, source_target_pairs={{0,1},{1,2},{2,3},{3,0},{4,5},{5,6},{6,7},{7,4},{8,9},{9,10},{10,1... | collective-permute-start | bytes 1376264 | tf_op jit(solution)/shard_map/ppermute | solution.py:28
  24.0 13.9 %copy-start.3 = (bf16[2,32,3584]{2,1,0:T(8,128)(2,1)}, bf16[2,32,3584]{2,1,0:T(8,128)(2,1)S(1)}, u32[]{:S(2)}) copy-start(bf16[2,32,3584]{2,1,0:T(8,128)(2,1)S(1)} %collective-permute-done) | copy-start | bytes 1376260
  24.0 13.6 %collective-permute-start.1 = (bf16[2,32,3584]{2,1,0:T(8,128)(2,1)S(1)}, bf16[2,32,3584]{2,1,0:T(8,128)(2,1)}, u32[]{:S(2)}, u32[]{:S(2)}) collective-permute-start(bf16[2,32,3584]{2,1,0:T(8,128)(2,1)S(1)} %collective-permute-done), channel_id=1, source_target_pairs={{0,1},{1,2},{2,3},{3,0},{4,5},{5,6},{6,7},{7,4},{8,9},{9,10},{10,1... | collective-permute-start | bytes 1376264 | tf_op jit(solution)/shard_map/ppermute | solution.py:28
  37.6 12.9 %collective-permute-start.2 = (bf16[2,32,3584]{2,1,0:T(8,128)(2,1)}, bf16[2,32,3584]{2,1,0:T(8,128)(2,1)}, u32[]{:S(2)}, u32[]{:S(2)}) collective-permute-start(bf16[2,32,3584]{2,1,0:T(8,128)(2,1)} %collective-permute-done.1), channel_id=1, source_target_pairs={{0,1},{1,2},{2,3},{3,0},{4,5},{5,6},{6,7},{7,4},{8,9},{9,10},{10,1... | collective-permute-start | bytes 1376264 | tf_op jit(solution)/shard_map/ppermute | solution.py:28
  38.4 17.6 %copy-start.4 = (bf16[2,32,3584]{2,1,0:T(8,128)(2,1)S(1)}, bf16[2,32,3584]{2,1,0:T(8,128)(2,1)}, u32[]{:S(2)}) copy-start(bf16[2,32,3584]{2,1,0:T(8,128)(2,1)} %copy-done.3) | copy-start | bytes 1376260
  53.8 34.5 %slice-start = ((s8[36700160]{0:T(1024)(128)(4,1)}), s8[3145728]{0:T(1024)(128)(4,1)S(1)}, s32[]{:S(2)}) async-start(s8[36700160]{0:T(1024)(128)(4,1)} %bitcast.207), calls=%async_computation.2 | async-start | bytes 6291456
  56.1 10.0 %copy-start.1 = (bf16[2,256,3584]{2,1,0:T(8,128)(2,1)}, bf16[2,256,3584]{2,1,0:T(8,128)(2,1)S(1)}, u32[]{:S(2)}) copy-start(bf16[2,256,3584]{2,1,0:T(8,128)(2,1)S(1)} %constant_dynamic-update-slice_fusion.2) | copy-start | bytes 11010052
  56.2 32.1 %slice-start.1 = ((s8[36700160]{0:T(1024)(128)(4,1)}), s8[4194304]{0:T(1024)(128)(4,1)S(1)}, s32[]{:S(2)}) async-start(s8[36700160]{0:T(1024)(128)(4,1)} %bitcast.207), calls=%async_computation.3 | async-start | bytes 8388608
  56.2 32.1 %slice-start.2 = ((s8[36700160]{0:T(1024)(128)(4,1)}), s8[4194304]{0:T(1024)(128)(4,1)S(1)}, s32[]{:S(2)}) async-start(s8[36700160]{0:T(1024)(128)(4,1)} %bitcast.207), calls=%async_computation.4 | async-start | bytes 8388608
  56.2 32.1 %slice-start.3 = ((s8[36700160]{0:T(1024)(128)(4,1)}), s8[4194304]{0:T(1024)(128)(4,1)S(1)}, s32[]{:S(2)}) async-start(s8[36700160]{0:T(1024)(128)(4,1)} %bitcast.207), calls=%async_computation.5 | async-start | bytes 8388608
  56.2 32.1 %slice-start.4 = ((s8[36700160]{0:T(1024)(128)(4,1)}), s8[4194304]{0:T(1024)(128)(4,1)S(1)}, s32[]{:S(2)}) async-start(s8[36700160]{0:T(1024)(128)(4,1)} %bitcast.207), calls=%async_computation.6 | async-start | bytes 8388608
  66.2 22.1 %slice-start.5 = ((s8[36700160]{0:T(1024)(128)(4,1)}), s8[4194304]{0:T(1024)(128)(4,1)S(1)}, s32[]{:S(2)}) async-start(s8[36700160]{0:T(1024)(128)(4,1)} %bitcast.207), calls=%async_computation.7 | async-start | bytes 8388608
  70.7 17.6 %slice-start.6 = ((s8[36700160]{0:T(1024)(128)(4,1)}), s8[4194304]{0:T(1024)(128)(4,1)S(1)}, s32[]{:S(2)}) async-start(s8[36700160]{0:T(1024)(128)(4,1)} %bitcast.207), calls=%async_computation.8 | async-start | bytes 8388608
  76.3 12.0 %slice-start.7 = ((s8[36700160]{0:T(1024)(128)(4,1)}), s8[4194304]{0:T(1024)(128)(4,1)S(1)}, s32[]{:S(2)}) async-start(s8[36700160]{0:T(1024)(128)(4,1)} %bitcast.207), calls=%async_computation.9 | async-start | bytes 8388608
  79.3 9.0 %slice-start.8 = ((s8[36700160]{0:T(1024)(128)(4,1)}), s8[4194304]{0:T(1024)(128)(4,1)S(1)}, s32[]{:S(2)}) async-start(s8[36700160]{0:T(1024)(128)(4,1)} %bitcast.207), calls=%async_computation.10 | async-start | bytes 8388608
  101.8 4.2 %copy-start.5 = (bf16[4,4,3584]{2,1,0:T(4,128)(2,1)S(1)}, bf16[4,4,3584]{2,1,0:T(4,128)(2,1)}, u32[]{:S(2)}) copy-start(bf16[4,4,3584]{2,1,0:T(4,128)(2,1)} %param.7) | copy-start | bytes 344068
  105.8 229.2 %all-gather.2.cloned.1.call-start = ((), (), s32[]{:S(2)}) async-start(), calls=%async_computation.1 | async-start | bytes 3784704 | tf_op jit(solution)/shard_map/all_gather | solution.py:21
  388.8 5.8 %copy-start = (f32[2,128,1024]{2,1,0:T(8,128)S(1)}, f32[2,128,1024]{2,1,0:T(8,128)}, u32[]{:S(2)}) copy-start(f32[2,128,1024]{2,1,0:T(8,128)} %get-tuple-element.17) | copy-start | bytes 3145732
  388.9 7.5 %copy-start.2 = (bf16[2,256,3584]{2,1,0:T(8,128)(2,1)S(1)}, bf16[2,256,3584]{2,1,0:T(8,128)(2,1)}, u32[]{:S(2)}) copy-start(bf16[2,256,3584]{2,1,0:T(8,128)(2,1)} %copy-done.1) | copy-start | bytes 11010052
Sparse Core Ops, SparseCore 0:
  105.9 165.0 all-reduce.1
  274.4 60.4 all-gather.1
